TPU v7x, 128 devices: a whole 4x4x4 slice. The times are simulated.
128 devices in a mesh: px: 8 (over x, core), py: 16 (over y, z).
Axes of the slice: x: 4, y: 4, z: 4, core: 2. Of those that a mesh axis runs over, the one named last changes fastest.
Arguments:
- cell_ids: int32 [131072, 128], P(('px', 'py')), may hold values from 0 to 32767
- masses: bfloat16 [131072, 128], P(('px', 'py')), may hold values from 0.5 to 2
- block_dest: int32 [131072, 1], P(('px', 'py')), may hold values from 0 to 1023; in each aligned block of 1024 rows (0 to 1023, 1024 to 2047, ...) at most 2 rows name the same one
- block_count: int32 [131072], P(('px', 'py')), may hold values from 1 to 128
- screen: float32 [8], replicated, may hold values from 0.02 to 0.2
Outputs:
- potential_modes: float32 [8, 128, 256], P(None, None, ('px', 'py'))
Inputs may be any that keep to these rules, and one draw needn't show every extreme that they name: `block_dest`: tile t lies on device t // 8 (devices numbered px-major) and plane t % 8. Among the 1024 blocks of one device no tile is named more than 2 times, a bound that some block reaches. `block_count`: the live particles of a block are its first ones. `cell_ids`: A cell c is row c // 128 and column c % (128) of the tile.
All inputs are finite; a program needn't handle non-finite values.
Results may differ from a plain program's by a relative error of at most 0.0003.
Values may be sent and summed in bfloat16 or wider, within the bound.
A program may use at most 64 MiB of HBM per device.

v0:
```python
import math
import jax
import jax.numpy as jnp
from jax import lax
from jax.sharding import PartitionSpec as P

NY = 2048
NZ = 2048
KY = 128
KZ = 128
CAP = 2
HIGHEST_PREC = lax.Precision.HIGHEST


def column_table(col_count):
    col_index = lax.broadcasted_iota(jnp.int32, (col_count, 2 * KZ), 0)
    col_slot = lax.broadcasted_iota(jnp.int32, (col_count, 2 * KZ), 1)
    col_freq = col_slot // 2 - KZ // 2
    col_phase = 2.0 * math.pi / NZ * jnp.remainder(col_freq * col_index, NZ).astype(jnp.float32)
    return jnp.where(col_slot % 2 == 0, jnp.cos(col_phase), -jnp.sin(col_phase))


def row_transform(row_coord, columns):
    y_freq = lax.broadcasted_iota(jnp.int32, row_coord.shape, 0) - KY // 2
    yphase = 2.0 * math.pi / NY * jnp.remainder(y_freq * row_coord, NY).astype(jnp.float32)
    cos_part = jnp.einsum("kp,lpc->lkc", jnp.cos(yphase), columns, precision=HIGHEST_PREC)
    sin_part = jnp.einsum("kp,lpc->lkc", jnp.sin(yphase), columns, precision=HIGHEST_PREC)
    real_part = cos_part[:, :, 0::2] + sin_part[:, :, 1::2]
    imag_part = cos_part[:, :, 1::2] - sin_part[:, :, 0::2]
    return jnp.stack([real_part, imag_part], axis=-1).reshape(
        columns.shape[0], row_coord.shape[0], columns.shape[2]
    )


def shards(cell_ids, masses, block_dest, block_count, screen):
    size_x = lax.axis_size("px")
    size_y = lax.axis_size("py")
    devices = size_x * size_y
    num_planes = screen.shape[0]
    blocks = cell_ids.shape[0]
    block_size = cell_ids.shape[1]
    tile_rows = NY // size_x
    tile_cols = NZ // size_y
    row_share = tile_rows // size_y
    col_share = 2 * KZ // devices
    num_tiles = devices * num_planes
    dest_tile = block_dest[:, 0]
    places = lax.broadcasted_iota(jnp.int32, (blocks, block_size), 1)
    weight = jnp.where(places < block_count[:, None], masses, jnp.zeros_like(masses))
    order_row = lax.broadcasted_iota(jnp.int32, (blocks, blocks), 0)
    order_col = lax.broadcasted_iota(jnp.int32, (blocks, blocks), 1)
    before = (dest_tile[:, None] == dest_tile[None, :]) & (order_col < order_row)
    slot_rank = jnp.sum(before.astype(jnp.int32), axis=1)
    owner_dev = dest_tile // num_planes
    plane_of = dest_tile % num_planes
    slot_index = (plane_of * devices + owner_dev) * CAP + slot_rank
    send_cells = jnp.zeros((num_tiles * CAP, block_size), jnp.int32).at[slot_index].set(cell_ids)
    send_mass = jnp.zeros((num_tiles * CAP, block_size), jnp.bfloat16).at[slot_index].set(weight)
    num_slots = devices * CAP * block_size
    send_cells = send_cells.reshape(num_planes, devices, CAP, block_size)
    send_mass = send_mass.reshape(num_planes, devices, CAP, block_size)
    recv_cells, recv_mass = (
        lax.all_to_all(send_cells, ("px", "py"), split_axis=1, concat_axis=1, tiled=True),
        lax.all_to_all(send_mass, ("px", "py"), split_axis=1, concat_axis=1, tiled=True),
    )
    plane_cells = recv_cells.reshape(num_planes, num_slots)
    plane_mass = recv_mass.reshape(num_planes, num_slots)

    def deposit(packed):
        cell_row, mass_row = packed
        row_of = cell_row // tile_cols
        col_of = cell_row % tile_cols
        row_iota = lax.broadcasted_iota(jnp.int32, (num_slots, tile_rows), 1)
        col_iota = lax.broadcasted_iota(jnp.int32, (num_slots, tile_cols), 1)
        onehot_rows = (row_iota == row_of[:, None]).astype(jnp.bfloat16)
        mass_cols = jnp.where(
            col_iota == col_of[:, None], mass_row[:, None], jnp.zeros((), jnp.bfloat16)
        )
        return lax.dot_general(
            onehot_rows, mass_cols, (((0,), (0,)), ((), ())), preferred_element_type=jnp.float32
        )

    density = lax.map(deposit, (plane_cells, plane_mass))
    z_slab = lax.all_to_all(density, "py", split_axis=1, concat_axis=2, tiled=True)
    ztable = column_table(NZ)
    spectra = jnp.dot(
        z_slab.reshape(num_planes * row_share, NZ),
        ztable,
        precision=HIGHEST_PREC,
        preferred_element_type=jnp.float32,
    )
    spectra = spectra.reshape(num_planes, row_share, 2 * KZ)
    positions = lax.broadcasted_iota(jnp.int32, (KY, NY), 1)
    columns = lax.all_to_all(spectra, ("px", "py"), split_axis=2, concat_axis=1, tiled=True)
    mode_values = row_transform(positions, columns)
    device = lax.axis_index("px") * size_y + lax.axis_index("py")
    z_mode = (
        device * col_share + lax.broadcasted_iota(jnp.int32, (KY, col_share), 1)
    ) // 2 - KZ // 2
    y_mode = lax.broadcasted_iota(jnp.int32, (KY, col_share), 0) - KY // 2
    wave_sq = (2.0 * jnp.sin(math.pi * y_mode.astype(jnp.float32) / NY)) ** 2 + (
        2.0 * jnp.sin(math.pi * z_mode.astype(jnp.float32) / NZ)
    ) ** 2
    is_zero = (y_mode == 0) & (z_mode == 0)
    scr = screen[:, None, None]
    green_fn = jnp.where(is_zero[None], jnp.zeros_like(wave_sq)[None], -scr / (wave_sq[None] + scr))
    return mode_values * green_fn * (1.0 / math.sqrt(NY * NZ))


def solution(mesh):
    return jax.shard_map(
        shards,
        mesh=mesh,
        in_specs=(
            P(("px", "py"), None),
            P(("px", "py"), None),
            P(("px", "py"), None),
            P(("px", "py")),
            P(),
        ),
        out_specs=P(None, None, ("px", "py")),
        check_vma=False,
    )
```

profile of v0, /device:TPU:1, one launch (start us, length us, event | category | flops | bytes accessed | tf_op | source)
XLA Modules:
  0.0 397.7 jit_solution(6626434158525641063)
XLA Ops:
  7.3 11.5 %all-to-all-start.1 = ((bf16[8,128,2,128]{3,2,0,1:T(2,128)(2,1)}), bf16[8,128,2,128]{3,2,0,1:T(2,128)(2,1)S(1)}, u32[]{:S(2)}, u32[]{:S(2)}) async-start(bf16[8,128,2,128]{3,2,0,1:T(2,128)(2,1)} %copy.31), calls=%async_computation.1 | async-start | bytes 1048576 | tf_op jit(solution)/shard_map/all_to_all | solution.py:64
  23.9 8.8 %all-to-all-done.1 = bf16[8,128,2,128]{3,2,0,1:T(2,128)(2,1)S(1)} async-done(((bf16[8,128,2,128]{3,2,0,1:T(2,128)(2,1)}), bf16[8,128,2,128]{3,2,0,1:T(2,128)(2,1)S(1)}, u32[]{:S(2)}, u32[]{:S(2)}) %all-to-all-start.1) | async-done | bytes 524320 | tf_op jit(solution)/shard_map/all_to_all | solution.py:64
  38.5 17.5 %all-to-all-done = s32[8,128,2,128]{3,2,0,1:T(2,128)S(1)} async-done(((s32[8,128,2,128]{3,2,0,1:T(2,128)}), s32[8,128,2,128]{3,2,0,1:T(2,128)S(1)}, u32[]{:S(2)}, u32[]{:S(2)}) %all-to-all-start) | async-done | bytes 1048608 | tf_op jit(solution)/shard_map/all_to_all | solution.py:63
  57.2 279.7 %while.12 = (s32[]{:T(128)}, f32[8,256,128]{2,0,1:T(8,128)}, s32[8,32768]{1,0:T(8,128)S(1)}, bf16[8,32768]{1,0:T(8,128)(2,1)}, s32[]{:T(128)}, /*index=5*/s32[]{:T(128)}) while((s32[]{:T(128)}, f32[8,256,128]{2,0,1:T(8,128)}, s32[8,32768]{1,0:T(8,128)S(1)}, bf16[8,32768]{1,0:T(8,128)(2,1)}, s32[]{:T(128)}, /*index=5*/s32[]{:T(128)}) %tuple.34), condition=%wide.region_4.5_spmd, body=%wide.region_3.4_spmd.sunk | while | flops 2164883456 | bytes 18284624 | solution.py:83
  59.4 12.0 %fusion.88 = bf16[32768,128]{1,0:T(8,128)(2,1)} fusion(s32[32768]{0:T(1024)S(1)} %get-tuple-element.110, bf16[32768]{0:T(1024)(128)(2,1)S(1)} %dynamic-slice_reduce_fusion.2), kind=kLoop, calls=%fused_computation.6.clone.clone.2.clone.1 | loop fusion | flops 8388608 | bytes 8585216 | tf_op jit(solution)/shard_map/while/body/eval_jaxpr/dot_general | solution.py:79
  71.4 16.6 %fusion.89 = f32[256,128]{1,0:T(8,128)S(1)} fusion(s32[32768]{0:T(1024)S(1)} %get-tuple-element.109, bf16[32768,128]{1,0:T(8,128)(2,1)} %fusion.88), kind=kOutput, calls=%fused_computation.3.clone.3 | convolution fusion | flops 2155872256 | bytes 8650752 | tf_op jit(solution)/shard_map/while/body/eval_jaxpr/dot_general | solution.py:79
  87.9 4.7 %dynamic_update_slice.8 = f32[8,256,128]{2,0,1:T(8,128)} dynamic-update-slice(f32[8,256,128]{2,0,1:T(8,128)} %get-tuple-element.118, f32[1,256,128]{2,0,1:T(1,128)S(1)} %bitcast.63, s32[]{:T(128)} %get-tuple-element.117, s32[]{:T(128)} %constant.176.clone.1..sunk, s32[]{:T(128)} %constant.176.clone.1..sunk) | dynamic-update-slice | bytes 262148 | tf_op jit(solution)/shard_map/while/body/jit(dynamic_update_index_in_dim)/dynamic_update_slice | solution.py:83
  94.3 12.0 %fusion.88 = bf16[32768,128]{1,0:T(8,128)(2,1)} fusion(s32[32768]{0:T(1024)S(1)} %get-tuple-element.110, bf16[32768]{0:T(1024)(128)(2,1)S(1)} %dynamic-slice_reduce_fusion.2), kind=kLoop, calls=%fused_computation.6.clone.clone.2.clone.1 | loop fusion | flops 8388608 | bytes 8585216 | tf_op jit(solution)/shard_map/while/body/eval_jaxpr/dot_general | solution.py:79
  106.3 16.6 %fusion.89 = f32[256,128]{1,0:T(8,128)S(1)} fusion(s32[32768]{0:T(1024)S(1)} %get-tuple-element.109, bf16[32768,128]{1,0:T(8,128)(2,1)} %fusion.88), kind=kOutput, calls=%fused_computation.3.clone.3 | convolution fusion | flops 2155872256 | bytes 8650752 | tf_op jit(solution)/shard_map/while/body/eval_jaxpr/dot_general | solution.py:79
  122.8 4.7 %dynamic_update_slice.8 = f32[8,256,128]{2,0,1:T(8,128)} dynamic-update-slice(f32[8,256,128]{2,0,1:T(8,128)} %get-tuple-element.118, f32[1,256,128]{2,0,1:T(1,128)S(1)} %bitcast.63, s32[]{:T(128)} %get-tuple-element.117, s32[]{:T(128)} %constant.176.clone.1..sunk, s32[]{:T(128)} %constant.176.clone.1..sunk) | dynamic-update-slice | bytes 262148 | tf_op jit(solution)/shard_map/while/body/jit(dynamic_update_index_in_dim)/dynamic_update_slice | solution.py:83
  129.2 12.0 %fusion.88 = bf16[32768,128]{1,0:T(8,128)(2,1)} fusion(s32[32768]{0:T(1024)S(1)} %get-tuple-element.110, bf16[32768]{0:T(1024)(128)(2,1)S(1)} %dynamic-slice_reduce_fusion.2), kind=kLoop, calls=%fused_computation.6.clone.clone.2.clone.1 | loop fusion | flops 8388608 | bytes 8585216 | tf_op jit(solution)/shard_map/while/body/eval_jaxpr/dot_general | solution.py:79
  141.1 16.6 %fusion.89 = f32[256,128]{1,0:T(8,128)S(1)} fusion(s32[32768]{0:T(1024)S(1)} %get-tuple-element.109, bf16[32768,128]{1,0:T(8,128)(2,1)} %fusion.88), kind=kOutput, calls=%fused_computation.3.clone.3 | convolution fusion | flops 2155872256 | bytes 8650752 | tf_op jit(solution)/shard_map/while/body/eval_jaxpr/dot_general | solution.py:79
  157.7 4.7 %dynamic_update_slice.8 = f32[8,256,128]{2,0,1:T(8,128)} dynamic-update-slice(f32[8,256,128]{2,0,1:T(8,128)} %get-tuple-element.118, f32[1,256,128]{2,0,1:T(1,128)S(1)} %bitcast.63, s32[]{:T(128)} %get-tuple-element.117, s32[]{:T(128)} %constant.176.clone.1..sunk, s32[]{:T(128)} %constant.176.clone.1..sunk) | dynamic-update-slice | bytes 262148 | tf_op jit(solution)/shard_map/while/body/jit(dynamic_update_index_in_dim)/dynamic_update_slice | solution.py:83
  164.0 12.0 %fusion.88 = bf16[32768,128]{1,0:T(8,128)(2,1)} fusion(s32[32768]{0:T(1024)S(1)} %get-tuple-element.110, bf16[32768]{0:T(1024)(128)(2,1)S(1)} %dynamic-slice_reduce_fusion.2), kind=kLoop, calls=%fused_computation.6.clone.clone.2.clone.1 | loop fusion | flops 8388608 | bytes 8585216 | tf_op jit(solution)/shard_map/while/body/eval_jaxpr/dot_general | solution.py:79
  176.0 16.6 %fusion.89 = f32[256,128]{1,0:T(8,128)S(1)} fusion(s32[32768]{0:T(1024)S(1)} %get-tuple-element.109, bf16[32768,128]{1,0:T(8,128)(2,1)} %fusion.88), kind=kOutput, calls=%fused_computation.3.clone.3 | convolution fusion | flops 2155872256 | bytes 8650752 | tf_op jit(solution)/shard_map/while/body/eval_jaxpr/dot_general | solution.py:79
  192.6 4.7 %dynamic_update_slice.8 = f32[8,256,128]{2,0,1:T(8,128)} dynamic-update-slice(f32[8,256,128]{2,0,1:T(8,128)} %get-tuple-element.118, f32[1,256,128]{2,0,1:T(1,128)S(1)} %bitcast.63, s32[]{:T(128)} %get-tuple-element.117, s32[]{:T(128)} %constant.176.clone.1..sunk, s32[]{:T(128)} %constant.176.clone.1..sunk) | dynamic-update-slice | bytes 262148 | tf_op jit(solution)/shard_map/while/body/jit(dynamic_update_index_in_dim)/dynamic_update_slice | solution.py:83
  198.9 12.0 %fusion.88 = bf16[32768,128]{1,0:T(8,128)(2,1)} fusion(s32[32768]{0:T(1024)S(1)} %get-tuple-element.110, bf16[32768]{0:T(1024)(128)(2,1)S(1)} %dynamic-slice_reduce_fusion.2), kind=kLoop, calls=%fused_computation.6.clone.clone.2.clone.1 | loop fusion | flops 8388608 | bytes 8585216 | tf_op jit(solution)/shard_map/while/body/eval_jaxpr/dot_general | solution.py:79
  210.9 16.6 %fusion.89 = f32[256,128]{1,0:T(8,128)S(1)} fusion(s32[32768]{0:T(1024)S(1)} %get-tuple-element.109, bf16[32768,128]{1,0:T(8,128)(2,1)} %fusion.88), kind=kOutput, calls=%fused_computation.3.clone.3 | convolution fusion | flops 2155872256 | bytes 8650752 | tf_op jit(solution)/shard_map/while/body/eval_jaxpr/dot_general | solution.py:79
  227.4 4.7 %dynamic_update_slice.8 = f32[8,256,128]{2,0,1:T(8,128)} dynamic-update-slice(f32[8,256,128]{2,0,1:T(8,128)} %get-tuple-element.118, f32[1,256,128]{2,0,1:T(1,128)S(1)} %bitcast.63, s32[]{:T(128)} %get-tuple-element.117, s32[]{:T(128)} %constant.176.clone.1..sunk, s32[]{:T(128)} %constant.176.clone.1..sunk) | dynamic-update-slice | bytes 262148 | tf_op jit(solution)/shard_map/while/body/jit(dynamic_update_index_in_dim)/dynamic_update_slice | solution.py:83
  233.8 12.0 %fusion.88 = bf16[32768,128]{1,0:T(8,128)(2,1)} fusion(s32[32768]{0:T(1024)S(1)} %get-tuple-element.110, bf16[32768]{0:T(1024)(128)(2,1)S(1)} %dynamic-slice_reduce_fusion.2), kind=kLoop, calls=%fused_computation.6.clone.clone.2.clone.1 | loop fusion | flops 8388608 | bytes 8585216 | tf_op jit(solution)/shard_map/while/body/eval_jaxpr/dot_general | solution.py:79
  245.8 16.6 %fusion.89 = f32[256,128]{1,0:T(8,128)S(1)} fusion(s32[32768]{0:T(1024)S(1)} %get-tuple-element.109, bf16[32768,128]{1,0:T(8,128)(2,1)} %fusion.88), kind=kOutput, calls=%fused_computation.3.clone.3 | convolution fusion | flops 2155872256 | bytes 8650752 | tf_op jit(solution)/shard_map/while/body/eval_jaxpr/dot_general | solution.py:79
  262.3 4.7 %dynamic_update_slice.8 = f32[8,256,128]{2,0,1:T(8,128)} dynamic-update-slice(f32[8,256,128]{2,0,1:T(8,128)} %get-tuple-element.118, f32[1,256,128]{2,0,1:T(1,128)S(1)} %bitcast.63, s32[]{:T(128)} %get-tuple-element.117, s32[]{:T(128)} %constant.176.clone.1..sunk, s32[]{:T(128)} %constant.176.clone.1..sunk) | dynamic-update-slice | bytes 262148 | tf_op jit(solution)/shard_map/while/body/jit(dynamic_update_index_in_dim)/dynamic_update_slice | solution.py:83
  268.7 12.0 %fusion.88 = bf16[32768,128]{1,0:T(8,128)(2,1)} fusion(s32[32768]{0:T(1024)S(1)} %get-tuple-element.110, bf16[32768]{0:T(1024)(128)(2,1)S(1)} %dynamic-slice_reduce_fusion.2), kind=kLoop, calls=%fused_computation.6.clone.clone.2.clone.1 | loop fusion | flops 8388608 | bytes 8585216 | tf_op jit(solution)/shard_map/while/body/eval_jaxpr/dot_general | solution.py:79
  280.7 16.6 %fusion.89 = f32[256,128]{1,0:T(8,128)S(1)} fusion(s32[32768]{0:T(1024)S(1)} %get-tuple-element.109, bf16[32768,128]{1,0:T(8,128)(2,1)} %fusion.88), kind=kOutput, calls=%fused_computation.3.clone.3 | convolution fusion | flops 2155872256 | bytes 8650752 | tf_op jit(solution)/shard_map/while/body/eval_jaxpr/dot_general | solution.py:79
  303.6 12.0 %fusion.88 = bf16[32768,128]{1,0:T(8,128)(2,1)} fusion(s32[32768]{0:T(1024)S(1)} %get-tuple-element.110, bf16[32768]{0:T(1024)(128)(2,1)S(1)} %dynamic-slice_reduce_fusion.2), kind=kLoop, calls=%fused_computation.6.clone.clone.2.clone.1 | loop fusion | flops 8388608 | bytes 8585216 | tf_op jit(solution)/shard_map/while/body/eval_jaxpr/dot_general | solution.py:79
  315.5 16.6 %fusion.89 = f32[256,128]{1,0:T(8,128)S(1)} fusion(s32[32768]{0:T(1024)S(1)} %get-tuple-element.109, bf16[32768,128]{1,0:T(8,128)(2,1)} %fusion.88), kind=kOutput, calls=%fused_computation.3.clone.3 | convolution fusion | flops 2155872256 | bytes 8650752 | tf_op jit(solution)/shard_map/while/body/eval_jaxpr/dot_general | solution.py:79
  340.8 15.1 %all-to-all-done.2 = f32[8,256,128]{2,0,1:T(8,128)S(1)} async-done(((f32[8,256,128]{2,0,1:T(8,128)}), f32[8,256,128]{2,0,1:T(8,128)S(1)}, u32[]{:S(2)}, u32[]{:S(2)}) %all-to-all-start.2) | async-done | bytes 1048608 | tf_op jit(solution)/shard_map/all_to_all | solution.py:84
  356.7 9.5 %fusion.14 = f32[8,16,256]{2,1,0:T(8,128)S(1)} fusion(f32[8,16,2048]{2,1,0:T(8,128)S(1)} %dot_general.17, s32[256]{0:T(256)S(1)} %get-tuple-element.74, s32[256]{0:T(256)S(1)} %get-tuple-element.79, s32[256]{0:T(256)S(1)} %get-tuple-element.75, s32[256]{0:T(256)S(1)} %get-tuple-element.78, pred[256]{0:T(512)(128)(4,1)S(1)} %get-tuple-element.76, ...), kind=kOutput, calls=%fused_computation.30 | convolution fusion | flops 815792128 | bytes 1184256 | tf_op jit(solution)/shard_map/dot_general | solution.py:86
  367.7 6.7 %all-to-all-start.3 = ((f32[128,1,256]{2,1,0:T(1,128)}), f32[128,1,256]{2,1,0:T(1,128)S(1)}, u32[]{:S(2)}, u32[]{:S(2)}) async-start(f32[128,1,256]{2,1,0:T(1,128)} %reshape.223), calls=%async_computation.3 | async-start | bytes 262144 | tf_op jit(solution)/shard_map/all_to_all | solution.py:94
  374.5 10.0 %all-to-all-done.3 = f32[128,1,256]{2,1,0:T(1,128)S(1)} async-done(((f32[128,1,256]{2,1,0:T(1,128)}), f32[128,1,256]{2,1,0:T(1,128)S(1)}, u32[]{:S(2)}, u32[]{:S(2)}) %all-to-all-start.3) | async-done | bytes 131104 | tf_op jit(solution)/shard_map/all_to_all | solution.py:94
  387.4 4.7 %convolution_bitcast_fusion = f32[8,128,2]{1,0,2:T(8,128)S(1)} fusion(f32[8,2048,2]{1,0,2:T(8,128)S(1)} %all_to_all.38, s32[128]{0:T(128)S(1)} %iota_add_fusion.1), kind=kOutput, calls=%fused_computation.43 | convolution fusion | flops 54001664 | bytes 139776 | tf_op jit(solution)/shard_map/kp,lpc->lkc/dot_general | solution.py:27
  392.1 4.7 %convolution_bitcast_fusion.1 = f32[8,128,2]{1,0,2:T(8,128)S(1)} fusion(f32[8,2048,2]{1,0,2:T(8,128)S(1)} %all_to_all.38, s32[128]{0:T(128)S(1)} %iota_add_fusion.1), kind=kOutput, calls=%fused_computation.44 | convolution fusion | flops 54001664 | bytes 139776 | tf_op jit(solution)/shard_map/kp,lpc->lkc/dot_general | solution.py:26
  (64 shorter events, 51.6 us)
Async XLA Ops:
  7.3 25.4 %all-to-all-start.1 = ((bf16[8,128,2,128]{3,2,0,1:T(2,128)(2,1)}), bf16[8,128,2,128]{3,2,0,1:T(2,128)(2,1)S(1)}, u32[]{:S(2)}, u32[]{:S(2)}) async-start(bf16[8,128,2,128]{3,2,0,1:T(2,128)(2,1)} %copy.31), calls=%async_computation.1 | async-start | bytes 1048576 | tf_op jit(solution)/shard_map/all_to_all | solution.py:64
  32.7 23.3 %all-to-all-start = ((s32[8,128,2,128]{3,2,0,1:T(2,128)}), s32[8,128,2,128]{3,2,0,1:T(2,128)S(1)}, u32[]{:S(2)}, u32[]{:S(2)}) async-start(s32[8,128,2,128]{3,2,0,1:T(2,128)} %copy.29), calls=%async_computation | async-start | bytes 2097152 | tf_op jit(solution)/shard_map/all_to_all | solution.py:63
  336.9 19.0 %all-to-all-start.2 = ((f32[8,256,128]{2,0,1:T(8,128)}), f32[8,256,128]{2,0,1:T(8,128)S(1)}, u32[]{:S(2)}, u32[]{:S(2)}) async-start(f32[8,256,128]{2,0,1:T(8,128)} %get-tuple-element.61), calls=%async_computation.2 | async-start | bytes 2097152 | tf_op jit(solution)/shard_map/all_to_all | solution.py:84
  366.2 8.3 %copy-start = (f32[8]{0:T(128)S(1)}, f32[8]{0:T(128)}, u32[]{:S(2)}) copy-start(f32[8]{0:T(128)} %param.11) | copy-start | bytes 100
  367.7 16.9 %all-to-all-start.3 = ((f32[128,1,256]{2,1,0:T(1,128)}), f32[128,1,256]{2,1,0:T(1,128)S(1)}, u32[]{:S(2)}, u32[]{:S(2)}) async-start(f32[128,1,256]{2,1,0:T(1,128)} %reshape.223), calls=%async_computation.3 | async-start | bytes 262144 | tf_op jit(solution)/shard_map/all_to_all | solution.py:94
where the time goes:
time: 405 us; the launch traced here: 398 us
  matrix products  151 us (37%)
  other arithmetic  104 us (26%)
  local copies, waits for them, and re-layouts  63.4 us (16%)
  waiting for transfers between devices  51.4 us (13%)
  starting transfers between devices  26.1 us (6%)
    dot_general x8, matrix products, deposit(): lax.dot_general(onehot_rows, mass_cols, (((0,), (0,)), ((), ())), preferr...  132 us
    dot_general x8, other arithmetic, deposit(): lax.dot_general(onehot_rows, mass_cols, (((0,), (0,)), ((), ())), preferr...  95.8 us
    dynamic_update_slice x8, local copies, waits for them, and re-layouts, shards(): density = lax.map(deposit, (plane_cells, plane_mass))  37.4 us
    all_to_all x1, waiting for transfers between devices, shards(): lax.all_to_all(send_cells, ('px', 'py'), split_axis=1, concat_axis=1, til...  17.5 us
    all_to_all x1, waiting for transfers between devices, shards(): lax.all_to_all(density, 'py', split_axis=1, concat_axis=2, tiled=True)  15.1 us
    dynamic_slice x16, local copies, waits for them, and re-layouts, shards(): density = lax.map(deposit, (plane_cells, plane_mass))  12.4 us
    all_to_all x1, starting transfers between devices, shards(): lax.all_to_all(send_mass, ('px', 'py'), split_axis=1, concat_axis=1, tile...  11.5 us
    all_to_all x1, waiting for transfers between devices, shards(): lax.all_to_all(spectra, ('px', 'py'), split_axis=2, concat_axis=1, tiled=...  10 us
  transfers between devices with their start and end apart: 4, of which 4 were waited for; matrix products, arithmetic and copies ran while one was open for 2% of the time, Pallas kernels for 0%

commit v1 on v0

--- a/solution.py
+++ b/solution.py
@@ -81,7 +81,11 @@
         )
 
     density = lax.map(deposit, (plane_cells, plane_mass))
-    z_slab = lax.all_to_all(density, "py", split_axis=1, concat_axis=2, tiled=True)
+    z = lax.axis_size("py")
+    e_now = jnp.split(density, z, 1)
+    u1 = jnp.stack(e_now)
+    built = lax.all_to_all(u1, "py", 0, 0)
+    z_slab = jnp.concatenate(built, 2)
     ztable = column_table(NZ)
     spectra = jnp.dot(
         z_slab.reshape(num_planes * row_share, NZ),

time: 405 us -> 387 us (0.956)
  local copies, waits for them, and re-layouts: 63.4 us -> 39.5 us
  matrix products: 151 us -> 157 us
    dynamic_update_slice x8 -> x0, local copies, waits for them, and re-layouts: 37.4 us -> none  [shards(): density = lax.map(deposit, (plane_cells, plane_mass))]
    unnamed x4 -> x19, local copies, waits for them, and re-layouts: 1.36 us -> 23.3 us
    dynamic_slice x16, local copies, waits for them, and re-layouts: 12.4 us -> 3.97 us  [shards(): density = lax.map(deposit, (plane_cells, plane_mass))]
    dot_general x8, matrix products: 132 us -> 138 us  [deposit(): lax.dot_general(onehot_rows, mass_cols, (((0,), (0,)), ((), ())), preferr...]
where the time goes in v1:
time: 387 us; the launch traced here: 380 us
  matrix products  157 us (41%)
  other arithmetic  104 us (27%)
  waiting for transfers between devices  52 us (13%)
  local copies, waits for them, and re-layouts  39.5 us (10%)
  starting transfers between devices  26.4 us (7%)
    dot_general x8, matrix products, deposit(): lax.dot_general(onehot_rows, mass_cols, (((0,), (0,)), ((), ())), preferr...  138 us
    dot_general x8, other arithmetic, deposit(): lax.dot_general(onehot_rows, mass_cols, (((0,), (0,)), ((), ())), preferr...  95.8 us
    unnamed x19, local copies, waits for them, and re-layouts  23.3 us
    all_to_all x1, waiting for transfers between devices, shards(): lax.all_to_all(send_cells, ('px', 'py'), split_axis=1, concat_axis=1, til...  18.3 us
    all_to_all x1, waiting for transfers between devices, shards(): built = lax.all_to_all(u1, 'py', 0, 0)  15.1 us
    all_to_all x1, starting transfers between devices, shards(): lax.all_to_all(send_mass, ('px', 'py'), split_axis=1, concat_axis=1, tile...  11.5 us
    all_to_all x1, waiting for transfers between devices, shards(): lax.all_to_all(spectra, ('px', 'py'), split_axis=2, concat_axis=1, tiled=...  9.87 us
    dot_general x1, matrix products, shards(): jnp.dot(z_slab.reshape(num_planes * row_share, NZ), ztable, precision=HIG...  9.55 us
  transfers between devices with their start and end apart: 4, of which 4 were waited for; matrix products, arithmetic and copies ran while one was open for 2% of the time, Pallas kernels for 0%

profile of v1, /device:TPU:1, one launch (start us, length us, event | category | flops | bytes accessed | tf_op | source)
XLA Modules:
  0.0 379.9 jit_solution(12098528041521756518)
XLA Ops:
  2.0 4.2 %scatter_custom_fusion.1 = bf16[2048,128]{1,0:T(8,128)(2,1)S(1)} fusion(s32[1024]{0:T(1024)S(1)} %bitcast.99, bf16[1024,128]{1,0:T(8,128)(2,1)} %param.8, s32[1024]{0:T(1024)} %param.10, bf16[]{:T(256)} %constant.186.clone.1), kind=kCustom, calls=%fused_computation.74 | custom fusion | flops 262144 | bytes 791552 | tf_op jit(solution)/shard_map/scatter | solution.py:58
  7.3 11.5 %all-to-all-start.1 = ((bf16[8,128,2,128]{3,2,0,1:T(2,128)(2,1)}), bf16[8,128,2,128]{3,2,0,1:T(2,128)(2,1)S(1)}, u32[]{:S(2)}, u32[]{:S(2)}) async-start(bf16[8,128,2,128]{3,2,0,1:T(2,128)(2,1)} %copy.29), calls=%async_computation.1 | async-start | bytes 1048576 | tf_op jit(solution)/shard_map/all_to_all | solution.py:64
  18.8 3.7 scatter_custom_fusion
  23.9 8.8 %all-to-all-done.1 = bf16[8,128,2,128]{3,2,0,1:T(2,128)(2,1)S(1)} async-done(((bf16[8,128,2,128]{3,2,0,1:T(2,128)(2,1)}), bf16[8,128,2,128]{3,2,0,1:T(2,128)(2,1)S(1)}, u32[]{:S(2)}, u32[]{:S(2)}) %all-to-all-start.1) | async-done | bytes 524320 | tf_op jit(solution)/shard_map/all_to_all | solution.py:64
  32.7 4.2 %all-to-all-start = ((s32[8,128,2,128]{3,2,0,1:T(2,128)}), s32[8,128,2,128]{3,2,0,1:T(2,128)S(1)}, u32[]{:S(2)}, u32[]{:S(2)}) async-start(s32[8,128,2,128]{3,2,0,1:T(2,128)} %copy.27), calls=%async_computation | async-start | bytes 2097152 | tf_op jit(solution)/shard_map/all_to_all | solution.py:63
  37.7 18.3 %all-to-all-done = s32[8,128,2,128]{3,2,0,1:T(2,128)S(1)} async-done(((s32[8,128,2,128]{3,2,0,1:T(2,128)}), s32[8,128,2,128]{3,2,0,1:T(2,128)S(1)}, u32[]{:S(2)}, u32[]{:S(2)}) %all-to-all-start) | async-done | bytes 1048608 | tf_op jit(solution)/shard_map/all_to_all | solution.py:63
  57.2 239.1 %while.12 = (s32[]{:T(128)}, f32[8,256,128]{2,1,0:T(8,128)}, s32[8,32768]{1,0:T(8,128)S(1)}, bf16[8,32768]{1,0:T(8,128)(2,1)S(1)}, s32[]{:T(128)}) while((s32[]{:T(128)}, f32[8,256,128]{2,1,0:T(8,128)}, s32[8,32768]{1,0:T(8,128)S(1)}, bf16[8,32768]{1,0:T(8,128)(2,1)S(1)}, s32[]{:T(128)}) %tuple.34), condition=%wide.region_4.5_spmd, body=%wide.region_3.4_spmd.sunk | while | flops 2164883456 | bytes 18022980 | solution.py:83
  58.3 12.0 %fusion.96 = bf16[32768,128]{1,0:T(8,128)(2,1)} fusion(s32[32768]{0:T(1024)S(1)} %get-tuple-element.110, bf16[32768]{0:T(1024)(128)(2,1)S(1)} %dynamic-slice_reduce_fusion.2), kind=kLoop, calls=%fused_computation.6.clone.clone.clone.clone.clone.clone.2.clone.1 | loop fusion | flops 8388608 | bytes 8585216 | tf_op jit(solution)/shard_map/while/body/eval_jaxpr/dot_general | solution.py:79
  70.3 17.2 %fusion.97 = f32[8,256,128]{2,1,0:T(8,128)} fusion(f32[8,256,128]{2,1,0:T(8,128)} %get-tuple-element.117, s32[]{:T(128)} %get-tuple-element.116, s32[32768]{0:T(1024)S(1)} %get-tuple-element.109, bf16[32768,128]{1,0:T(8,128)(2,1)} %fusion.96), kind=kOutput, calls=%fused_computation.11.clone.3 | convolution fusion | flops 2155872256 | bytes 8651264 | tf_op jit(solution)/shard_map/while/body/eval_jaxpr/dot_general | solution.py:79
  88.2 12.0 %fusion.96 = bf16[32768,128]{1,0:T(8,128)(2,1)} fusion(s32[32768]{0:T(1024)S(1)} %get-tuple-element.110, bf16[32768]{0:T(1024)(128)(2,1)S(1)} %dynamic-slice_reduce_fusion.2), kind=kLoop, calls=%fused_computation.6.clone.clone.clone.clone.clone.clone.2.clone.1 | loop fusion | flops 8388608 | bytes 8585216 | tf_op jit(solution)/shard_map/while/body/eval_jaxpr/dot_general | solution.py:79
  100.1 17.2 %fusion.97 = f32[8,256,128]{2,1,0:T(8,128)} fusion(f32[8,256,128]{2,1,0:T(8,128)} %get-tuple-element.117, s32[]{:T(128)} %get-tuple-element.116, s32[32768]{0:T(1024)S(1)} %get-tuple-element.109, bf16[32768,128]{1,0:T(8,128)(2,1)} %fusion.96), kind=kOutput, calls=%fused_computation.11.clone.3 | convolution fusion | flops 2155872256 | bytes 8651264 | tf_op jit(solution)/shard_map/while/body/eval_jaxpr/dot_general | solution.py:79
  118.0 12.0 %fusion.96 = bf16[32768,128]{1,0:T(8,128)(2,1)} fusion(s32[32768]{0:T(1024)S(1)} %get-tuple-element.110, bf16[32768]{0:T(1024)(128)(2,1)S(1)} %dynamic-slice_reduce_fusion.2), kind=kLoop, calls=%fused_computation.6.clone.clone.clone.clone.clone.clone.2.clone.1 | loop fusion | flops 8388608 | bytes 8585216 | tf_op jit(solution)/shard_map/while/body/eval_jaxpr/dot_general | solution.py:79
  130.0 17.2 %fusion.97 = f32[8,256,128]{2,1,0:T(8,128)} fusion(f32[8,256,128]{2,1,0:T(8,128)} %get-tuple-element.117, s32[]{:T(128)} %get-tuple-element.116, s32[32768]{0:T(1024)S(1)} %get-tuple-element.109, bf16[32768,128]{1,0:T(8,128)(2,1)} %fusion.96), kind=kOutput, calls=%fused_computation.11.clone.3 | convolution fusion | flops 2155872256 | bytes 8651264 | tf_op jit(solution)/shard_map/while/body/eval_jaxpr/dot_general | solution.py:79
  147.8 12.0 %fusion.96 = bf16[32768,128]{1,0:T(8,128)(2,1)} fusion(s32[32768]{0:T(1024)S(1)} %get-tuple-element.110, bf16[32768]{0:T(1024)(128)(2,1)S(1)} %dynamic-slice_reduce_fusion.2), kind=kLoop, calls=%fused_computation.6.clone.clone.clone.clone.clone.clone.2.clone.1 | loop fusion | flops 8388608 | bytes 8585216 | tf_op jit(solution)/shard_map/while/body/eval_jaxpr/dot_general | solution.py:79
  159.8 17.2 %fusion.97 = f32[8,256,128]{2,1,0:T(8,128)} fusion(f32[8,256,128]{2,1,0:T(8,128)} %get-tuple-element.117, s32[]{:T(128)} %get-tuple-element.116, s32[32768]{0:T(1024)S(1)} %get-tuple-element.109, bf16[32768,128]{1,0:T(8,128)(2,1)} %fusion.96), kind=kOutput, calls=%fused_computation.11.clone.3 | convolution fusion | flops 2155872256 | bytes 8651264 | tf_op jit(solution)/shard_map/while/body/eval_jaxpr/dot_general | solution.py:79
  177.6 12.0 %fusion.96 = bf16[32768,128]{1,0:T(8,128)(2,1)} fusion(s32[32768]{0:T(1024)S(1)} %get-tuple-element.110, bf16[32768]{0:T(1024)(128)(2,1)S(1)} %dynamic-slice_reduce_fusion.2), kind=kLoop, calls=%fused_computation.6.clone.clone.clone.clone.clone.clone.2.clone.1 | loop fusion | flops 8388608 | bytes 8585216 | tf_op jit(solution)/shard_map/while/body/eval_jaxpr/dot_general | solution.py:79
  189.6 17.2 %fusion.97 = f32[8,256,128]{2,1,0:T(8,128)} fusion(f32[8,256,128]{2,1,0:T(8,128)} %get-tuple-element.117, s32[]{:T(128)} %get-tuple-element.116, s32[32768]{0:T(1024)S(1)} %get-tuple-element.109, bf16[32768,128]{1,0:T(8,128)(2,1)} %fusion.96), kind=kOutput, calls=%fused_computation.11.clone.3 | convolution fusion | flops 2155872256 | bytes 8651264 | tf_op jit(solution)/shard_map/while/body/eval_jaxpr/dot_general | solution.py:79
  207.4 12.0 %fusion.96 = bf16[32768,128]{1,0:T(8,128)(2,1)} fusion(s32[32768]{0:T(1024)S(1)} %get-tuple-element.110, bf16[32768]{0:T(1024)(128)(2,1)S(1)} %dynamic-slice_reduce_fusion.2), kind=kLoop, calls=%fused_computation.6.clone.clone.clone.clone.clone.clone.2.clone.1 | loop fusion | flops 8388608 | bytes 8585216 | tf_op jit(solution)/shard_map/while/body/eval_jaxpr/dot_general | solution.py:79
  219.4 17.2 %fusion.97 = f32[8,256,128]{2,1,0:T(8,128)} fusion(f32[8,256,128]{2,1,0:T(8,128)} %get-tuple-element.117, s32[]{:T(128)} %get-tuple-element.116, s32[32768]{0:T(1024)S(1)} %get-tuple-element.109, bf16[32768,128]{1,0:T(8,128)(2,1)} %fusion.96), kind=kOutput, calls=%fused_computation.11.clone.3 | convolution fusion | flops 2155872256 | bytes 8651264 | tf_op jit(solution)/shard_map/while/body/eval_jaxpr/dot_general | solution.py:79
  237.2 12.0 %fusion.96 = bf16[32768,128]{1,0:T(8,128)(2,1)} fusion(s32[32768]{0:T(1024)S(1)} %get-tuple-element.110, bf16[32768]{0:T(1024)(128)(2,1)S(1)} %dynamic-slice_reduce_fusion.2), kind=kLoop, calls=%fused_computation.6.clone.clone.clone.clone.clone.clone.2.clone.1 | loop fusion | flops 8388608 | bytes 8585216 | tf_op jit(solution)/shard_map/while/body/eval_jaxpr/dot_general | solution.py:79
  249.2 17.2 %fusion.97 = f32[8,256,128]{2,1,0:T(8,128)} fusion(f32[8,256,128]{2,1,0:T(8,128)} %get-tuple-element.117, s32[]{:T(128)} %get-tuple-element.116, s32[32768]{0:T(1024)S(1)} %get-tuple-element.109, bf16[32768,128]{1,0:T(8,128)(2,1)} %fusion.96), kind=kOutput, calls=%fused_computation.11.clone.3 | convolution fusion | flops 2155872256 | bytes 8651264 | tf_op jit(solution)/shard_map/while/body/eval_jaxpr/dot_general | solution.py:79
  267.0 12.0 %fusion.96 = bf16[32768,128]{1,0:T(8,128)(2,1)} fusion(s32[32768]{0:T(1024)S(1)} %get-tuple-element.110, bf16[32768]{0:T(1024)(128)(2,1)S(1)} %dynamic-slice_reduce_fusion.2), kind=kLoop, calls=%fused_computation.6.clone.clone.clone.clone.clone.clone.2.clone.1 | loop fusion | flops 8388608 | bytes 8585216 | tf_op jit(solution)/shard_map/while/body/eval_jaxpr/dot_general | solution.py:79
  279.0 17.2 %fusion.97 = f32[8,256,128]{2,1,0:T(8,128)} fusion(f32[8,256,128]{2,1,0:T(8,128)} %get-tuple-element.117, s32[]{:T(128)} %get-tuple-element.116, s32[32768]{0:T(1024)S(1)} %get-tuple-element.109, bf16[32768,128]{1,0:T(8,128)(2,1)} %fusion.96), kind=kOutput, calls=%fused_computation.11.clone.3 | convolution fusion | flops 2155872256 | bytes 8651264 | tf_op jit(solution)/shard_map/while/body/eval_jaxpr/dot_general | solution.py:79
  302.2 1.5 bitcast_dynamic-update-slice_fusion.11
  316.9 1.5 bitcast_dynamic-update-slice_fusion.1
  319.8 3.7 all-to-all-start.2
  323.7 15.1 %all-to-all-done.2 = f32[16,8,16,128]{3,2,1,0:T(8,128)S(1)} async-done(((f32[16,8,16,128]{3,2,1,0:T(8,128)}), f32[16,8,16,128]{3,2,1,0:T(8,128)S(1)}, u32[]{:S(2)}, u32[]{:S(2)}) %all-to-all-start.2) | async-done | bytes 1048608 | tf_op jit(solution)/shard_map/all_to_all | solution.py:87
  338.8 9.5 %fusion.20 = f32[8,16,256]{2,1,0:T(8,128)S(1)} fusion(s32[256]{0:T(256)S(1)} %get-tuple-element.74, s32[256]{0:T(256)S(1)} %get-tuple-element.79, s32[256]{0:T(256)S(1)} %get-tuple-element.75, s32[256]{0:T(256)S(1)} %get-tuple-element.78, pred[256]{0:T(512)(128)(4,1)S(1)} %get-tuple-element.76, pred[256]{0:T(512)(128)(4,1)S(1)} %get-tuple-element.77, ...), kind=kOutput, calls=%fused_computation.32 | convolution fusion | flops 815792128 | bytes 1184256 | tf_op jit(solution)/shard_map/dot_general | solution.py:90
  349.8 7.0 %all-to-all-start.3 = ((f32[128,1,256]{2,1,0:T(1,128)}), f32[128,1,256]{2,1,0:T(1,128)S(1)}, u32[]{:S(2)}, u32[]{:S(2)}) async-start(f32[128,1,256]{2,1,0:T(1,128)} %reshape.225), calls=%async_computation.3 | async-start | bytes 262144 | tf_op jit(solution)/shard_map/all_to_all | solution.py:98
  356.9 9.9 %all-to-all-done.3 = f32[128,1,256]{2,1,0:T(1,128)S(1)} async-done(((f32[128,1,256]{2,1,0:T(1,128)}), f32[128,1,256]{2,1,0:T(1,128)S(1)}, u32[]{:S(2)}, u32[]{:S(2)}) %all-to-all-start.3) | async-done | bytes 131104 | tf_op jit(solution)/shard_map/all_to_all | solution.py:98
  369.6 4.7 %convolution_bitcast_fusion = f32[8,128,2]{1,0,2:T(8,128)S(1)} fusion(f32[8,2048,2]{1,0,2:T(8,128)S(1)} %all_to_all.28, s32[128]{0:T(128)S(1)} %iota_add_fusion.1), kind=kOutput, calls=%fused_computation.45 | convolution fusion | flops 54001664 | bytes 139776 | tf_op jit(solution)/shard_map/kp,lpc->lkc/dot_general | solution.py:27
  374.3 4.7 %convolution_bitcast_fusion.1 = f32[8,128,2]{1,0,2:T(8,128)S(1)} fusion(f32[8,2048,2]{1,0,2:T(8,128)S(1)} %all_to_all.28, s32[128]{0:T(128)S(1)} %iota_add_fusion.1), kind=kOutput, calls=%fused_computation.46 | convolution fusion | flops 54001664 | bytes 139776 | tf_op jit(solution)/shard_map/kp,lpc->lkc/dot_general | solution.py:26
  (70 shorter events, 37.0 us)
Async XLA Ops:
  7.3 25.4 %all-to-all-start.1 = ((bf16[8,128,2,128]{3,2,0,1:T(2,128)(2,1)}), bf16[8,128,2,128]{3,2,0,1:T(2,128)(2,1)S(1)}, u32[]{:S(2)}, u32[]{:S(2)}) async-start(bf16[8,128,2,128]{3,2,0,1:T(2,128)(2,1)} %copy.29), calls=%async_computation.1 | async-start | bytes 1048576 | tf_op jit(solution)/shard_map/all_to_all | solution.py:64
  32.7 23.3 %all-to-all-start = ((s32[8,128,2,128]{3,2,0,1:T(2,128)}), s32[8,128,2,128]{3,2,0,1:T(2,128)S(1)}, u32[]{:S(2)}, u32[]{:S(2)}) async-start(s32[8,128,2,128]{3,2,0,1:T(2,128)} %copy.27), calls=%async_computation | async-start | bytes 2097152 | tf_op jit(solution)/shard_map/all_to_all | solution.py:63
  319.8 19.0 %all-to-all-start.2 = ((f32[16,8,16,128]{3,2,1,0:T(8,128)}), f32[16,8,16,128]{3,2,1,0:T(8,128)S(1)}, u32[]{:S(2)}, u32[]{:S(2)}) async-start(f32[16,8,16,128]{3,2,1,0:T(8,128)} %bitcast_dynamic-update-slice_fusion), calls=%async_computation.2 | async-start | bytes 2097152 | tf_op jit(solution)/shard_map/all_to_all | solution.py:87
  348.3 8.6 %copy-start = (f32[8]{0:T(128)S(1)}, f32[8]{0:T(128)}, u32[]{:S(2)}) copy-start(f32[8]{0:T(128)} %param.11) | copy-start | bytes 100
  349.8 17.0 %all-to-all-start.3 = ((f32[128,1,256]{2,1,0:T(1,128)}), f32[128,1,256]{2,1,0:T(1,128)S(1)}, u32[]{:S(2)}, u32[]{:S(2)}) async-start(f32[128,1,256]{2,1,0:T(1,128)} %reshape.225), calls=%async_computation.3 | async-start | bytes 262144 | tf_op jit(solution)/shard_map/all_to_all | solution.py:98
